TPU v7x, 256 devices: a whole 4x4x8 slice. The times are simulated.
256 devices in a mesh: lat: 8 (over z_lo, core), lon: 8 (over z_hi, x), chan: 4 (over y).
Axes of the slice: x: 4, y: 4, z: 8 (z_hi: 2, z_lo: 4; z = z_hi * 4 + z_lo), core: 2. Of those that a mesh axis runs over, the one named last changes fastest.
Arguments:
- queries: bfloat16 [128, 64, 2560], P('lat', 'lon', 'chan'), may hold values from -8 to 8
- keys: bfloat16 [128, 64, 2560], P('lat', 'lon', 'chan'), may hold values from -8 to 8
- values: bfloat16 [128, 64, 2560], P('lat', 'lon', 'chan'), may hold values from -6 to 6
- attn_out: bfloat16 [128, 64, 2560], P('lat', 'lon', 'chan'), may hold values from -6 to 6
- grad_out: bfloat16 [128, 64, 5120], P('lat', 'lon', 'chan'), may hold values from -6 to 6
- w_out: bfloat16 [5120, 2560], P(('lat', 'lon'), 'chan'), may hold values from -0.078125 to 0.078125
- bias_table: float32 [20, 25, 13], P('chan'), may hold values from -5 to 5
- key_mask: int32 [128, 64], replicated, may hold values 0 or 1
Outputs:
- grad_queries: bfloat16 [128, 64, 2560], P('lat', 'lon', 'chan')
- grad_keys: bfloat16 [128, 64, 2560], P('lat', 'lon', 'chan')
- grad_values: bfloat16 [128, 64, 2560], P('lat', 'lon', 'chan')
- grad_wout: float32 [5120, 2560], P(('lat', 'lon'), 'chan')
- grad_table: float32 [20, 25, 13], P('chan')
All inputs are finite; a program needn't handle non-finite values.
Results may differ from a plain program's by a relative error of at most 0.007.
Values may be sent and summed in bfloat16 or wider, within the bound.
No kernel may reach another device: no remote copies, remote signals or barrier semaphores. Data moves between devices by JAX's collectives and lax.ppermute only.
A program may use at most 128 MiB of HBM per device.

v0:
```python
import jax
import jax.numpy as jnp
from jax import lax
from jax.sharding import PartitionSpec as P

HEAD_DIM = 128
WIN = 13


def extended_2(value, sides, width, wrap):
    for axis, dim in sides:
        count, length = (lax.axis_size(axis), value.shape[dim])
        up = [(i, (i + 1) % count) for i in range(count if wrap else count - 1)]
        down = [(j, i) for i, j in up]
        last = lax.slice_in_dim(value, length - width, length, axis=dim)
        leading = lax.slice_in_dim(value, 0, width, axis=dim)
        before = lax.ppermute(last, axis, up)
        after = lax.ppermute(leading, axis, down)
        value = jnp.concatenate([before, value, after], axis=dim)
    return value


def fold_lon(extended, core_width):
    full_width = extended.shape[2]
    reach_cells = (full_width - core_width) // 2
    rim_cells = jnp.concatenate(
        [extended[:, :, :reach_cells], extended[:, :, full_width - reach_cells :]], axis=2
    )
    received = extended_2(rim_cells.astype(jnp.bfloat16), (("lon", 2),), reach_cells, True).astype(
        rim_cells.dtype
    )
    middle = extended[:, :, reach_cells : full_width - reach_cells]
    front_add = jnp.pad(
        received[:, :, :reach_cells], ((0, 0), (0, 0), (0, core_width - reach_cells), (0, 0))
    )
    back_add = jnp.pad(
        received[:, :, 3 * reach_cells :], ((0, 0), (0, 0), (core_width - reach_cells, 0), (0, 0))
    )
    return middle + front_add + back_add


def fold_lat(extended, core_width):
    full_width = extended.shape[1]
    reach_cells = (full_width - core_width) // 2
    rim_cells = jnp.concatenate(
        [extended[:, :reach_cells], extended[:, full_width - reach_cells :]], axis=1
    )
    received = extended_2(rim_cells.astype(jnp.bfloat16), (("lat", 1),), reach_cells, False).astype(
        rim_cells.dtype
    )
    middle = extended[:, reach_cells : full_width - reach_cells]
    front_add = jnp.pad(
        received[:, :reach_cells], ((0, 0), (0, core_width - reach_cells), (0, 0), (0, 0))
    )
    back_add = jnp.pad(
        received[:, 3 * reach_cells :], ((0, 0), (core_width - reach_cells, 0), (0, 0), (0, 0))
    )
    return middle + front_add + back_add


def local(queries, keys, values, attn_out, grad_out, w_out, bias_table, key_mask):
    lat_rows, lon_cols, chan_width = queries.shape
    head_count = bias_table.shape[0]
    reach_cells = WIN // 2
    score_scale = HEAD_DIM ** (-0.5)
    tokens = lat_rows * lon_cols
    ext_rows = lat_rows + 2 * reach_cells
    ext_cols = lon_cols + 2 * reach_cells
    row_block = 4
    key_span = row_block + WIN - 1
    block_count = lat_rows // row_block
    block_rows = row_block * lon_cols
    block_keys = key_span * ext_cols
    offset_rows = 2 * WIN - 1
    low_pad = row_block - 1
    lat_total = lat_rows * lax.axis_size("lat")
    lon_total = lon_cols * lax.axis_size("lon")
    contract_lead = (((0,), (0,)), ((), ()))
    full_grad = lax.all_gather(grad_out, "chan", axis=2, tiled=True).reshape(tokens, -1)
    grad_cols = jnp.transpose(full_grad)
    slab_part = grad_cols
    grad_attn = lax.dot_general(
        slab_part,
        lax.all_gather(w_out, ("lat", "lon"), axis=0, tiled=True),
        contract_lead,
        preferred_element_type=jnp.float32,
    ).astype(jnp.bfloat16)
    kv_pair = jnp.stack([keys, values])
    extended = extended_2(kv_pair, (("lat", 1), ("lon", 2)), reach_cells, True)
    lat_first = lax.axis_index("lat") * lat_rows
    lon_first = lax.axis_index("lon") * lon_cols
    ext_col = lon_first - reach_cells + jnp.arange(ext_cols, dtype=jnp.int32)
    wrap_col = ext_col % lon_total
    mask_cols = jnp.take(key_mask, wrap_col, axis=1)
    mark_cols = wrap_col % 4 == 0
    rel_lon = (
        jnp.arange(ext_cols, dtype=jnp.int32)[None, :]
        - jnp.arange(lon_cols, dtype=jnp.int32)[:, None]
    )
    in_lon = (rel_lon >= 0) & (rel_lon < WIN)
    lon_pick = jnp.clip(rel_lon, 0, WIN - 1)
    lon_table = jnp.take(bias_table, lon_pick, axis=2).transpose(0, 2, 1, 3)
    table_pad = jnp.pad(lon_table, ((0, 0), (0, 0), (low_pad, low_pad), (0, 0)))
    query_heads = queries.reshape(lat_rows, lon_cols, head_count, HEAD_DIM)
    grad_heads = grad_attn.reshape(lat_rows, lon_cols, head_count, HEAD_DIM)

    def block_step(state_pair, block_index):
        grad_pair, table_acc = state_pair
        local_first = block_index * row_block
        top_row = lat_first + local_first
        key_first = jnp.clip(top_row - reach_cells, 0, lat_total - key_span)
        key_local = key_first - (lat_first - reach_cells)
        query_rows = top_row + jnp.arange(row_block, dtype=jnp.int32)
        window_first = jnp.clip(query_rows - reach_cells, 0, lat_total - WIN)
        key_glob = key_first + jnp.arange(key_span, dtype=jnp.int32)
        in_lat = (key_glob[None, :] >= window_first[:, None]) & (
            key_glob[None, :] < window_first[:, None] + WIN
        )
        mask_rows = lax.dynamic_slice_in_dim(mask_cols, key_first, key_span, 0)
        valid_keys = (mask_rows == 1) | (key_glob % 4 == 0)[:, None] & mark_cols[None, :]
        allowed = in_lat[:, None, :, None] & in_lon[None, :, None, :] & valid_keys[None, None, :, :]
        allowed = allowed.reshape(block_rows, block_keys)
        shifts = key_first - query_rows + (WIN - 1) + low_pad
        bias_parts = [
            lax.dynamic_slice_in_dim(table_pad, shifts[row_pos], key_span, 2)
            for row_pos in range(row_block)
        ]
        bias_rows = jnp.stack(bias_parts, axis=1).reshape(head_count, block_rows, block_keys)
        query_block = lax.dynamic_slice_in_dim(query_heads, local_first, row_block, 0).reshape(
            block_rows, head_count, HEAD_DIM
        )
        grad_block = lax.dynamic_slice_in_dim(grad_heads, local_first, row_block, 0).reshape(
            block_rows, head_count, HEAD_DIM
        )
        pair_block = lax.dynamic_slice_in_dim(extended, key_local, key_span, 1).reshape(
            2, block_keys, head_count, HEAD_DIM
        )
        key_block = pair_block[0]
        value_block = pair_block[1]
        scores = (
            score_scale
            * jnp.einsum("qhd,khd->hqk", query_block, key_block, preferred_element_type=jnp.float32)
            + bias_rows
        )
        scores = jnp.where(allowed[None], scores, -1e30)
        row_max = jnp.max(scores, axis=2, keepdims=True)
        weights_exp = jnp.exp(scores - row_max)
        prob_rows = weights_exp / jnp.sum(weights_exp, axis=2, keepdims=True)
        grad_prob = jnp.einsum(
            "qhd,khd->hqk", grad_block, value_block, preferred_element_type=jnp.float32
        )
        row_delta = jnp.sum(prob_rows * grad_prob, axis=2, keepdims=True)
        dscore = prob_rows * (grad_prob - row_delta)
        score_grid = dscore.reshape(head_count, row_block, lon_cols, key_span, ext_cols)
        score_grid = score_grid.transpose(0, 1, 3, 2, 4).reshape(
            head_count, row_block, key_span, lon_cols * ext_cols
        )
        for row_pos in range(row_block):
            prior_sum = lax.dynamic_slice_in_dim(table_acc, shifts[row_pos], key_span, 1)
            table_acc = lax.dynamic_update_slice_in_dim(
                table_acc, prior_sum + score_grid[:, row_pos], shifts[row_pos], 1
            )
        dscore_low = dscore.astype(jnp.bfloat16)
        prob_low = prob_rows.astype(jnp.bfloat16)
        grad_query = (
            score_scale
            * jnp.einsum("hqk,khd->qhd", dscore_low, key_block, preferred_element_type=jnp.float32)
        ).astype(jnp.bfloat16)
        key_part = score_scale * jnp.einsum(
            "hqk,qhd->khd", dscore_low, query_block, preferred_element_type=jnp.float32
        )
        value_part = jnp.einsum(
            "hqk,qhd->khd", prob_low, grad_block, preferred_element_type=jnp.float32
        )
        new_part = jnp.stack([key_part, value_part]).reshape(2, key_span, ext_cols, chan_width)
        prior_pair = lax.dynamic_slice_in_dim(grad_pair, key_local, key_span, 1)
        grad_pair = lax.dynamic_update_slice_in_dim(grad_pair, prior_pair + new_part, key_local, 1)
        return ((grad_pair, table_acc), grad_query)

    zero_pair = jnp.zeros((2, ext_rows, ext_cols, chan_width), jnp.float32)
    zero_table = jnp.zeros(
        (head_count, offset_rows + 2 * low_pad, lon_cols * ext_cols), jnp.float32
    )
    (grad_pair, table_acc), query_blocks = lax.scan(
        block_step, (zero_pair, zero_table), jnp.arange(block_count, dtype=jnp.int32)
    )
    grad_queries = query_blocks.reshape(lat_rows, lon_cols, chan_width)
    table_core = table_acc[:, low_pad : low_pad + offset_rows].reshape(
        head_count, offset_rows, lon_cols, ext_cols
    )
    col_take = (
        jnp.arange(lon_cols, dtype=jnp.int32)[:, None] + jnp.arange(WIN, dtype=jnp.int32)[None, :]
    )
    col_take = jnp.broadcast_to(
        col_take[None, None, :, :], (head_count, offset_rows, lon_cols, WIN)
    )
    table_local = jnp.sum(jnp.take_along_axis(table_core, col_take, axis=3), axis=2)
    grad_table = lax.psum(table_local, ("lat", "lon"))
    folded = fold_lat(fold_lon(grad_pair, lon_cols), lat_rows)
    grad_keys = folded[0].astype(jnp.bfloat16)
    grad_values = folded[1].astype(jnp.bfloat16)
    saved_out = attn_out.reshape(tokens, chan_width)
    slab_part = grad_cols
    grad_wout = lax.psum_scatter(
        jnp.dot(slab_part, saved_out, preferred_element_type=jnp.float32),
        ("lat", "lon"),
        scatter_dimension=0,
        tiled=True,
    )
    return (grad_queries, grad_keys, grad_values, grad_wout, grad_table)


def solution(mesh):
    return jax.shard_map(
        local,
        mesh=mesh,
        in_specs=(
            P("lat", "lon", "chan"),
            P("lat", "lon", "chan"),
            P("lat", "lon", "chan"),
            P("lat", "lon", "chan"),
            P("lat", "lon", "chan"),
            P(("lat", "lon"), "chan"),
            P("chan", None, None),
            P(),
        ),
        out_specs=(
            P("lat", "lon", "chan"),
            P("lat", "lon", "chan"),
            P("lat", "lon", "chan"),
            P(("lat", "lon"), "chan"),
            P("chan", None, None),
        ),
        check_vma=False,
    )
```

profile of v0, /device:TPU:240, one launch (start us, length us, event | category | flops | bytes accessed | tf_op | source)
XLA Modules:
  0.0 933.4 jit_solution(14924076082434811027)
XLA Ops:
  7.2 1.8 copy.63
  9.8 26.9 %all-gather.3.cloned.1.call-done = bf16[16,8,5120]{2,0,1:T(8,128)(2,1)} async-done(((bf16[16,8,1280]{2,0,1:T(8,128)(2,1)}), bf16[16,8,5120]{2,0,1:T(8,128)(2,1)}) %all-gather.3.cloned.1.call-update) | async-done | bytes 1310736 | tf_op jit(solution)/shard_map/all_gather | solution.py:79
  36.7 7.9 convolution_bitcast_fusion.1
  44.7 0.9 copy-done.9
  45.8 1.7 collective-permute-start.1
  49.0 1.0 collective-permute-done
  51.5 4.6 collective-permute-start.3
  56.1 1.4 gather_fusion.1
  58.2 0.9 pad.20.clone
  59.1 11.4 %collective-permute-done.3 = bf16[2,28,6,640]{3,0,2,1:T(2,128)(2,1)S(1)} collective-permute-done((bf16[2,28,6,640]{3,0,2,1:T(2,128)(2,1)S(1)}, bf16[2,28,6,640]{3,0,2,1:T(2,128)(2,1)S(1)}, u32[]{:S(2)}, u32[]{:S(2)}) %collective-permute-start.3) | collective-permute-done | bytes 430112 | tf_op jit(solution)/shard_map/ppermute | solution.py:18
  70.6 10.3 %collective-permute-done.2 = bf16[2,28,6,640]{3,0,2,1:T(2,128)(2,1)S(1)} collective-permute-done((bf16[2,28,6,640]{3,0,2,1:T(2,128)(2,1)S(1)}, bf16[2,28,6,640]{3,0,2,1:T(2,128)(2,1)S(1)}, u32[]{:S(2)}, u32[]{:S(2)}) %collective-permute-start.2) | collective-permute-done | bytes 430112 | tf_op jit(solution)/shard_map/ppermute | solution.py:17
  80.9 2.1 pad_maximum_fusion.1
  83.0 156.4 %all-gather.5.cloned.1.call-done = bf16[5120,640]{1,0:T(8,128)(2,1)} async-done(((bf16[80,640]{1,0:T(8,128)(2,1)}), bf16[5120,640]{1,0:T(8,128)(2,1)}) %all-gather.5.cloned.1.call-update) | async-done | bytes 6553616 | tf_op jit(solution)/shard_map/all_gather | solution.py:84
  239.4 4.6 fusion.42
  244.0 1.9 broadcast_in_dim.94
  245.9 117.0 %while.18 = (s32[]{:T(128)}, f32[2,28,20,640]{3,2,1,0:T(8,128)}, f32[5,31,160]{2,1,0:T(8,128)S(1)}, bf16[4,32,5,128]{3,1,2,0:T(8,128)(2,1)}, s32[4]{0:T(128)S(1)...) while((s32[]{:T(128)}, f32[2,28,20,640]{3,2,1,0:T(8,128)}, ...), condition=%wide.region_4.5_spmd.clone, body=%wide.region_0.0_spmd.clone.sunk | while | flops 67648624 | bytes 32509632 | solution.py:184
  247.3 0.8 fusion.102
  257.6 1.3 constant_dynamic-slice_fusion.7
  259.8 1.9 dynamic-slice_bitcast_fusion.5
  262.7 0.9 fusion.104
  264.0 0.8 fusion.111
  265.9 1.2 stack.66
  268.0 1.2 stack.67
  269.2 0.8 reshape.367
  272.1 3.0 fusion.106
  286.0 0.8 constant_dynamic-slice_fusion.6
  286.8 1.3 constant_dynamic-slice_fusion.7
  289.0 1.9 dynamic-slice_bitcast_fusion.5
  291.9 0.9 fusion.104
  293.3 0.8 fusion.111
  295.2 1.2 stack.66
  297.2 1.2 stack.67
  298.4 0.8 reshape.367
  301.4 3.0 fusion.106
  305.8 0.8 fusion.102
  316.0 1.3 constant_dynamic-slice_fusion.7
  318.3 1.9 dynamic-slice_bitcast_fusion.5
  321.1 0.9 fusion.104
  322.5 0.8 fusion.111
  324.4 1.2 stack.66
  326.4 1.2 stack.67
  327.6 0.8 reshape.367
  330.6 3.1 fusion.106
  335.0 0.8 fusion.102
  345.3 1.3 constant_dynamic-slice_fusion.7
  347.5 1.9 dynamic-slice_bitcast_fusion.5
  350.4 0.9 fusion.104
  351.8 0.8 fusion.111
  353.6 1.2 stack.66
  355.7 1.2 stack.67
  356.9 0.8 reshape.367
  359.8 3.1 fusion.106
  363.0 2.2 convert.16
  365.3 1.1 copy.70
  366.5 1.1 copy.71
  367.6 2.0 collective-permute-start.4
  370.2 0.9 reshape.332
  371.3 155.3 %gather_fusion.2 = f32[13000]{0:T(1024)S(1)} fusion(f32[5,25,8,20]{3,2,1,0:T(8,128)S(1)} %reshape.333, s32[13000]{0:T(1024)S(1)} %reshape.350), kind=kCustom, calls=%fused_computation.2 | custom fusion | bytes 312000 | tf_op jit(solution)/shard_map/jit(take_along_axis)/gather | solution.py:197
  527.0 1.1 copy.73
  528.1 1.1 copy.72
  529.9 2.3 fusion.59
  532.3 2.1 collective-permute-start.6
  534.3 4.4 collective-permute-start.7
  539.0 386.1 %psum.7 = f32[5,25,13]{2,1,0:T(8,128)S(1)} all-reduce(f32[5,25,13]{2,1,0:T(8,128)S(1)} %select_reduce_fusion), channel_id=1, replica_groups=mesh['lat'=8,'lon'=8,'chan'=4] {'lat','lon'}, use_global_device_ids=true, to_apply=%region_7.8 | all-reduce | flops 1625 | bytes 13000 | tf_op jit(solution)/shard_map/psum | solution.py:198
  (265 shorter events, 44.5 us)
Async XLA Ops:
  7.2 29.5 %copy-start = (bf16[16,8,640]{2,1,0:T(8,128)(2,1)S(1)}, bf16[16,8,640]{2,1,0:T(8,128)(2,1)}, u32[]{:S(2)}) copy-start(bf16[16,8,640]{2,1,0:T(8,128)(2,1)} %param.13) | copy-start | bytes 491524
  7.2 29.5 %all-gather.3.cloned.1.call-start = ((), (), s32[]{:S(2)}) async-start(), calls=%async_computation.1 | async-start | bytes 1638400 | tf_op jit(solution)/shard_map/all_gather | solution.py:79
  9.0 230.4 %all-gather.5.cloned.1.call-start = ((), (), s32[]{:S(2)}) async-start(), calls=%async_computation.2 | async-start | bytes 6656000 | tf_op jit(solution)/shard_map/all_gather | solution.py:84
  9.8 917.1 %reduce-scatter.2.cloned.1.call-start = ((), (), s32[]{:S(2)}) async-start(), calls=%async_computation.3 | async-start | bytes 13312000 | tf_op jit(solution)/shard_map/reduce_scatter | solution.py:204
  44.6 0.9 copy-start.9
  44.6 1.0 copy-start.10
  44.6 3.0 copy-start.8
  45.7 4.4 collective-permute-start
  45.8 4.8 collective-permute-start.1
  50.6 5.5 copy-start.1
  51.5 19.0 %collective-permute-start.3 = (bf16[2,28,6,640]{3,0,2,1:T(2,128)(2,1)S(1)}, bf16[2,28,6,640]{3,0,2,1:T(2,128)(2,1)S(1)}, u32[]{:S(2)}, u32[]{:S(2)}) collective-permute-start(bf16[2,28,6,640]{3,0,2,1:T(2,128)(2,1)S(1)} %copy.59), channel_id=1, source_target_pairs={{4,0},{8,4},{12,8},{16,12},{20,16},{24,20},{28,24},{0,28},{5,1},{9... | collective-permute-start | bytes 1290248 | tf_op jit(solution)/shard_map/ppermute | solution.py:18
  56.1 24.7 %collective-permute-start.2 = (bf16[2,28,6,640]{3,0,2,1:T(2,128)(2,1)S(1)}, bf16[2,28,6,640]{3,0,2,1:T(2,128)(2,1)S(1)}, u32[]{:S(2)}, u32[]{:S(2)}) collective-permute-start(bf16[2,28,6,640]{3,0,2,1:T(2,128)(2,1)S(1)} %copy.58), channel_id=1, source_target_pairs={{0,4},{4,8},{8,12},{12,16},{16,20},{20,24},{24,28},{28,0},{1,5},{5... | collective-permute-start | bytes 1290248 | tf_op jit(solution)/shard_map/ppermute | solution.py:17
  80.9 158.5 %copy-start.11 = (bf16[16,8,5120]{2,0,1:T(8,128)(2,1)S(1)}, bf16[16,8,5120]{2,0,1:T(8,128)(2,1)}, u32[]{:S(2)}) copy-start(bf16[16,8,5120]{2,0,1:T(8,128)(2,1)} %all-gather.3.cloned.1.call-done) | copy-start | bytes 3932164
  245.9 13.4 %copy-start.12 = (bf16[16,8,5,128]{3,1,2,0:T(8,128)(2,1)}, bf16[16,8,5,128]{3,1,2,0:T(8,128)(2,1)S(1)}, u32[]{:S(2)}) copy-start(bf16[16,8,5,128]{3,1,2,0:T(8,128)(2,1)S(1)} %get-tuple-element.541) | copy-start | bytes 491524 | tf_op jit(solution)/shard_map/while
  270.5 1.5 copy-start.2
  270.9 1.3 copy-start.3
  272.1 3.0 copy-start.13
  275.2 13.4 %copy-start.12 = (bf16[16,8,5,128]{3,1,2,0:T(8,128)(2,1)}, bf16[16,8,5,128]{3,1,2,0:T(8,128)(2,1)S(1)}, u32[]{:S(2)}) copy-start(bf16[16,8,5,128]{3,1,2,0:T(8,128)(2,1)S(1)} %get-tuple-element.541) | copy-start | bytes 491524 | tf_op jit(solution)/shard_map/while
  299.7 1.5 copy-start.2
  300.1 1.3 copy-start.3
  301.4 3.0 copy-start.13
  304.4 13.4 %copy-start.12 = (bf16[16,8,5,128]{3,1,2,0:T(8,128)(2,1)}, bf16[16,8,5,128]{3,1,2,0:T(8,128)(2,1)S(1)}, u32[]{:S(2)}) copy-start(bf16[16,8,5,128]{3,1,2,0:T(8,128)(2,1)S(1)} %get-tuple-element.541) | copy-start | bytes 491524 | tf_op jit(solution)/shard_map/while
  328.9 1.5 copy-start.2
  329.3 1.3 copy-start.3
  330.6 3.1 copy-start.13
  333.6 13.4 %copy-start.12 = (bf16[16,8,5,128]{3,1,2,0:T(8,128)(2,1)}, bf16[16,8,5,128]{3,1,2,0:T(8,128)(2,1)S(1)}, u32[]{:S(2)}) copy-start(bf16[16,8,5,128]{3,1,2,0:T(8,128)(2,1)S(1)} %get-tuple-element.541) | copy-start | bytes 491524 | tf_op jit(solution)/shard_map/while
  358.2 1.5 copy-start.2
  358.6 1.3 copy-start.3
  359.8 3.1 copy-start.13
  365.3 4.3 copy-start.4
  365.3 4.3 copy-start.6
  365.3 4.7 copy-start.14
  367.6 159.4 %collective-permute-start.5 = (bf16[2,28,6,640]{3,0,2,1:T(2,128)(2,1)}, bf16[2,28,6,640]{3,0,2,1:T(2,128)(2,1)}, u32[]{:S(2)}, u32[]{:S(2)}) collective-permute-start(bf16[2,28,6,640]{3,0,2,1:T(2,128)(2,1)} %copy.71), channel_id=1, source_target_pairs={{4,0},{8,4},{12,8},{16,12},{20,16},{24,20},{28,24},{0,28},{5,1},{9... | collective-permute-start | bytes 1290248 | tf_op jit(solution)/shard_map/ppermute | solution.py:18
  367.6 160.5 %collective-permute-start.4 = (bf16[2,28,6,640]{3,0,2,1:T(2,128)(2,1)}, bf16[2,28,6,640]{3,0,2,1:T(2,128)(2,1)}, u32[]{:S(2)}, u32[]{:S(2)}) collective-permute-start(bf16[2,28,6,640]{3,0,2,1:T(2,128)(2,1)} %copy.70), channel_id=1, source_target_pairs={{0,4},{4,8},{8,12},{12,16},{16,20},{20,24},{24,28},{28,0},{1,5},{5... | collective-permute-start | bytes 1290248 | tf_op jit(solution)/shard_map/ppermute | solution.py:17
  369.6 1.7 copy-start.19
  369.6 1.7 copy-start.15
  369.6 1.7 copy-start.17
  526.6 2.6 copy-start.5
  526.6 2.6 copy-start.7
  529.2 0.7 copy-start.21
  529.9 8.9 copy-start.16
  529.9 8.9 copy-start.18
  529.9 8.9 copy-start.20
  532.2 393.8 %copy-start.22 = (pred[16]{0:T(512)(128)(4,1)S(1)}, pred[16]{0:T(512)(128)(4,1)}, u32[]{:S(2)}) copy-start(pred[16]{0:T(512)(128)(4,1)} %constant.227.clone.1) | copy-start | bytes 52
  532.3 393.6 %collective-permute-start.6 = (bf16[2,6,8,640]{3,2,1,0:T(8,128)(2,1)S(1)}, bf16[2,6,8,640]{3,2,1,0:T(8,128)(2,1)S(1)}, u32[]{:S(2)}, u32[]{:S(2)}) collective-permute-start(bf16[2,6,8,640]{3,2,1,0:T(8,128)(2,1)S(1)} %get-tuple-element.361), channel_id=1, source_target_pairs={{0,32},{32,64},{64,96},{96,128},{128,160},{160,192},{192,224},{1,3... | collective-permute-start | bytes 368648 | tf_op jit(solution)/shard_map/ppermute | solution.py:17
  534.3 391.5 %collective-permute-start.7 = (bf16[2,6,8,640]{3,2,1,0:T(8,128)(2,1)S(1)}, bf16[2,6,8,640]{3,2,1,0:T(8,128)(2,1)S(1)}, u32[]{:S(2)}, u32[]{:S(2)}) collective-permute-start(bf16[2,6,8,640]{3,2,1,0:T(8,128)(2,1)S(1)} %get-tuple-element.362), channel_id=1, source_target_pairs={{32,0},{64,32},{96,64},{128,96},{160,128},{192,160},{224,192},{33,... | collective-permute-start | bytes 368648 | tf_op jit(solution)/shard_map/ppermute | solution.py:18
Sparse Core Ops, SparseCore 0:
  9.8 26.8 all-gather.2
  38.5 200.8 all-gather.4
  242.6 461.3 reduce-scatter.1
where the time goes:
time: 935 us; the launch traced here: 933 us
  blocking collectives  386 us (41%)
  local copies, waits for them, and re-layouts  227 us (24%)
  waiting for transfers between devices  207 us (22%)
  loops' own time  33.7 us (4%)
  other arithmetic  28.7 us (3%)
  matrix products  21.7 us (2%)
  starting transfers between devices  15.1 us (2%)
  between operations  14.2 us (2%)
    psum x1, blocking collectives, local(): grad_table = lax.psum(table_local, ('lat', 'lon'))  386 us
    all_gather x1, waiting for transfers between devices, local(): lax.all_gather(w_out, ('lat', 'lon'), axis=0, tiled=True)  156 us
    gather x3, local copies, waits for them, and re-layouts, local(): jnp.take_along_axis(table_core, col_take, axis=3)  156 us
    another operation x1, loops' own time, local(): lax.scan(block_step, (zero_pair, zero_table), jnp.arange(block_count, dty...  33.7 us
    all_gather x1, waiting for transfers between devices, local(): lax.all_gather(grad_out, 'chan', axis=2, tiled=True).reshape(tokens, -1)  26.9 us
  transfers between devices with their start and end apart: 11, of which 6 were waited for; matrix products, arithmetic and copies ran while one was open for 29% of the time, Pallas kernels for 0%

commit v1 on v0

--- a/solution.py
+++ b/solution.py
@@ -5,6 +5,12 @@
 
 HEAD_DIM = 128
 WIN = 13
+
+
+def summed_here(x, mesh_axis):
+    shards = lax.all_gather(x, mesh_axis, axis=0, tiled=False)
+    total = shards.sum(axis=0)
+    return total
 
 
 def extended_2(value, sides, width, wrap):
@@ -195,7 +201,7 @@
         col_take[None, None, :, :], (head_count, offset_rows, lon_cols, WIN)
     )
     table_local = jnp.sum(jnp.take_along_axis(table_core, col_take, axis=3), axis=2)
-    grad_table = lax.psum(table_local, ("lat", "lon"))
+    grad_table = summed_here(table_local, ("lat", "lon"))
     folded = fold_lat(fold_lon(grad_pair, lon_cols), lat_rows)
     grad_keys = folded[0].astype(jnp.bfloat16)
     grad_values = folded[1].astype(jnp.bfloat16)

time: 935 us -> 802 us (0.86)
  blocking collectives: 386 us -> 248 us
    psum x1 -> x0, blocking collectives: 386 us -> none  [local(): grad_table = lax.psum(table_local, ('lat', 'lon'))]
    all_gather x0 -> x1, blocking collectives: none -> 248 us  [summed_here(): shards = lax.all_gather(x, mesh_axis, axis=0, tiled=False)]
  transfers between devices with their start and end apart: 11 -> 11, of which waited for: 6 -> 5; matrix products, arithmetic and copies ran while one was open for 29% -> 34% of each run, Pallas kernels for 0% -> 0%
where the time goes in v1:
time: 802 us; the launch traced here: 793 us
  blocking collectives  248 us (31%)
  local copies, waits for them, and re-layouts  226 us (28%)
  waiting for transfers between devices  209 us (26%)
  loops' own time  34.3 us (4%)
  other arithmetic  27.9 us (3%)
  matrix products  20 us (2%)
  starting transfers between devices  14.4 us (2%)
  between operations  14.1 us (2%)
    all_gather x1, blocking collectives, summed_here(): shards = lax.all_gather(x, mesh_axis, axis=0, tiled=False)  248 us
    all_gather x1, waiting for transfers between devices, local(): lax.all_gather(w_out, ('lat', 'lon'), axis=0, tiled=True)  156 us
    gather x3, local copies, waits for them, and re-layouts, local(): jnp.take_along_axis(table_core, col_take, axis=3)  156 us
    another operation x1, loops' own time, local(): lax.scan(block_step, (zero_pair, zero_table), jnp.arange(block_count, dty...  34.3 us
    all_gather x1, waiting for transfers between devices, local(): lax.all_gather(grad_out, 'chan', axis=2, tiled=True).reshape(tokens, -1)  26.9 us
  transfers between devices with their start and end apart: 11, of which 5 were waited for; matrix products, arithmetic and copies ran while one was open for 34% of the time, Pallas kernels for 0%

profile of v1, /device:TPU:240, one launch (start us, length us, event | category | flops | bytes accessed | tf_op | source)
XLA Modules:
  0.0 793.0 jit_solution(16007302181598063708)
XLA Ops:
  7.2 1.8 copy.85
  9.1 0.7 all-gather.6.cloned.1.call-update
  9.8 26.9 %all-gather.4.cloned.1.call-done = bf16[16,8,5120]{2,0,1:T(8,128)(2,1)} async-done(((bf16[16,8,1280]{2,0,1:T(8,128)(2,1)}), bf16[16,8,5120]{2,0,1:T(8,128)(2,1)}) %all-gather.4.cloned.1.call-update) | async-done | bytes 1310736 | tf_op jit(solution)/shard_map/all_gather | solution.py:85
  36.7 7.9 %convolution_bitcast_fusion.1 = f32[5120,640]{1,0:T(8,128)} fusion(bf16[16,8,5120]{2,0,1:T(8,128)(2,1)} %all-gather.4.cloned.1.call-done, bf16[16,8,640]{2,1,0:T(8,128)(2,1)S(1)} %copy-done), kind=kOutput, calls=%fused_computation.77 | convolution fusion | flops 838860800 | bytes 14581760 | tf_op jit(solution)/shard_map/dot_general | solution.py:211
  44.7 0.9 copy-done.11
  45.8 1.7 collective-permute-start.1
  48.4 1.4 gather_fusion.1
  51.5 4.8 collective-permute-start.3
  56.5 0.9 pad.20.clone
  57.5 12.8 %collective-permute-done.3 = bf16[2,28,6,640]{3,0,2,1:T(2,128)(2,1)S(1)} collective-permute-done((bf16[2,28,6,640]{3,0,2,1:T(2,128)(2,1)S(1)}, bf16[2,28,6,640]{3,0,2,1:T(2,128)(2,1)S(1)}, u32[]{:S(2)}, u32[]{:S(2)}) %collective-permute-start.3) | collective-permute-done | bytes 430112 | tf_op jit(solution)/shard_map/ppermute | solution.py:24
  70.4 11.9 %collective-permute-done.2 = bf16[2,28,6,640]{3,0,2,1:T(2,128)(2,1)S(1)} collective-permute-done((bf16[2,28,6,640]{3,0,2,1:T(2,128)(2,1)S(1)}, bf16[2,28,6,640]{3,0,2,1:T(2,128)(2,1)S(1)}, u32[]{:S(2)}, u32[]{:S(2)}) %collective-permute-start.2) | collective-permute-done | bytes 430112 | tf_op jit(solution)/shard_map/ppermute | solution.py:23
  82.4 2.1 pad_maximum_fusion.1
  84.4 156.1 %all-gather.6.cloned.1.call-done = bf16[5120,640]{1,0:T(8,128)(2,1)} async-done(((bf16[80,640]{1,0:T(8,128)(2,1)}), bf16[5120,640]{1,0:T(8,128)(2,1)}) %all-gather.6.cloned.1.call-update) | async-done | bytes 6553616 | tf_op jit(solution)/shard_map/all_gather | solution.py:90
  240.5 5.2 fusion.42
  245.7 1.9 broadcast_in_dim.94
  247.7 112.3 %while.18 = (s32[]{:T(128)}, f32[2,28,20,640]{3,2,1,0:T(8,128)}, f32[5,31,160]{2,1,0:T(8,128)S(1)}, bf16[4,32,5,128]{3,1,2,0:T(8,128)(2,1)S(1)}, s32[4]{0:T(128)...) while((s32[]{:T(128)}, f32[2,28,20,640]{3,2,1,0:T(8,128)}, ...), condition=%wide.region_4.5_spmd.clone, body=%wide.region_0.0_spmd.clone.sunk | while | flops 67648624 | bytes 32878328 | solution.py:190
  257.9 0.8 constant_dynamic-slice_fusion.6
  258.7 1.3 constant_dynamic-slice_fusion.7
  260.9 1.9 dynamic-slice_bitcast_fusion.5
  263.8 0.9 fusion.104
  266.5 1.2 stack.66
  268.5 1.2 stack.67
  269.7 0.8 reshape.368
  272.7 3.1 fusion.106
  277.4 0.6 fusion.98
  286.0 0.8 constant_dynamic-slice_fusion.6
  286.8 1.3 constant_dynamic-slice_fusion.7
  289.0 1.9 dynamic-slice_bitcast_fusion.5
  291.9 0.9 fusion.104
  294.5 1.2 stack.66
  296.6 1.2 stack.67
  297.8 0.8 reshape.368
  300.8 3.1 fusion.106
  314.0 0.8 constant_dynamic-slice_fusion.6
  314.8 1.3 constant_dynamic-slice_fusion.7
  317.1 1.9 dynamic-slice_bitcast_fusion.5
  319.9 0.9 fusion.104
  322.6 1.2 stack.66
  324.6 1.2 stack.67
  325.8 0.8 reshape.368
  328.8 3.1 fusion.106
  342.1 0.8 constant_dynamic-slice_fusion.6
  342.9 1.3 constant_dynamic-slice_fusion.7
  345.1 1.9 dynamic-slice_bitcast_fusion.5
  348.0 0.9 fusion.104
  350.7 1.2 stack.66
  352.7 1.2 stack.67
  353.9 0.8 reshape.368
  356.9 3.1 fusion.106
  360.0 2.2 convert.16
  362.4 1.2 copy.92
  363.6 1.1 copy.93
  364.6 2.0 collective-permute-start.4
  367.2 0.9 reshape.332
  368.3 155.1 %gather_fusion.2 = f32[13000]{0:T(1024)S(1)} fusion(f32[5,25,8,20]{3,2,1,0:T(8,128)S(1)} %reshape.333, s32[13000]{0:T(1024)S(1)} %reshape.350), kind=kCustom, calls=%fused_computation.2 | custom fusion | bytes 312000 | tf_op jit(solution)/shard_map/jit(take_along_axis)/gather | solution.py:203
  524.1 1.1 copy.95
  525.2 1.1 copy.94
  526.9 3.3 fusion.59
  530.3 1.9 collective-permute-start.6
  532.2 3.7 collective-permute-start.7
  535.9 247.6 %all-gather = f32[320,25,13]{1,2,0:T(8,128)S(1)} all-gather(f32[5,25,13]{1,2,0:T(8,128)S(1)} %copy.97), channel_id=2, replica_groups=mesh['lat'=8,'lon'=8,'chan'=4] {'lat','lon'}, dimensions={0}, use_global_device_ids=true | all-gather | bytes 422500 | tf_op jit(solution)/shard_map/all_gather | solution.py:11
  783.4 0.9 reduce_sum.45
  784.5 1.1 copy-done.10
  785.7 0.8 slice_bitcast_fusion.4
  (272 shorter events, 38.7 us)
Async XLA Ops:
  7.2 29.5 %copy-start = (bf16[16,8,640]{2,1,0:T(8,128)(2,1)S(1)}, bf16[16,8,640]{2,1,0:T(8,128)(2,1)}, u32[]{:S(2)}) copy-start(bf16[16,8,640]{2,1,0:T(8,128)(2,1)} %param.13) | copy-start | bytes 491524
  7.2 29.5 %all-gather.4.cloned.1.call-start = ((), (), s32[]{:S(2)}) async-start(), calls=%async_computation.1 | async-start | bytes 1638400 | tf_op jit(solution)/shard_map/all_gather | solution.py:85
  9.0 231.5 %all-gather.6.cloned.1.call-start = ((), (), s32[]{:S(2)}) async-start(), calls=%async_computation.2 | async-start | bytes 6656000 | tf_op jit(solution)/shard_map/all_gather | solution.py:90
  9.8 776.7 %reduce-scatter.2.cloned.1.call-start = ((), (), s32[]{:S(2)}) async-start(), calls=%async_computation.3 | async-start | bytes 13312000 | tf_op jit(solution)/shard_map/reduce_scatter | solution.py:210
  44.7 0.9 copy-start.11
  44.7 1.0 copy-start.12
  44.7 2.9 copy-start.9
  44.7 3.7 copy-start.2
  45.7 4.6 collective-permute-start
  45.8 4.8 collective-permute-start.1
  51.5 18.8 %collective-permute-start.3 = (bf16[2,28,6,640]{3,0,2,1:T(2,128)(2,1)S(1)}, bf16[2,28,6,640]{3,0,2,1:T(2,128)(2,1)S(1)}, u32[]{:S(2)}, u32[]{:S(2)}) collective-permute-start(bf16[2,28,6,640]{3,0,2,1:T(2,128)(2,1)S(1)} %copy.81), channel_id=1, source_target_pairs={{4,0},{8,4},{12,8},{16,12},{20,16},{24,20},{28,24},{0,28},{5,1},{9... | collective-permute-start | bytes 1290248 | tf_op jit(solution)/shard_map/ppermute | solution.py:24
  56.4 25.9 %collective-permute-start.2 = (bf16[2,28,6,640]{3,0,2,1:T(2,128)(2,1)S(1)}, bf16[2,28,6,640]{3,0,2,1:T(2,128)(2,1)S(1)}, u32[]{:S(2)}, u32[]{:S(2)}) collective-permute-start(bf16[2,28,6,640]{3,0,2,1:T(2,128)(2,1)S(1)} %copy.80), channel_id=1, source_target_pairs={{0,4},{4,8},{8,12},{12,16},{16,20},{20,24},{24,28},{28,0},{1,5},{5... | collective-permute-start | bytes 1290248 | tf_op jit(solution)/shard_map/ppermute | solution.py:23
  82.3 158.2 %copy-start.13 = (bf16[16,8,5120]{2,0,1:T(8,128)(2,1)S(1)}, bf16[16,8,5120]{2,0,1:T(8,128)(2,1)}, u32[]{:S(2)}) copy-start(bf16[16,8,5120]{2,0,1:T(8,128)(2,1)} %all-gather.4.cloned.1.call-done) | copy-start | bytes 3932164
  247.7 12.3 %copy-start.14 = (s32[128,20]{1,0:T(8,128)}, s32[128,20]{1,0:T(8,128)S(1)}, u32[]{:S(2)}) copy-start(s32[128,20]{1,0:T(8,128)S(1)} %get-tuple-element.541) | copy-start | bytes 30724 | tf_op jit(solution)/shard_map/while
  265.4 2.3 copy-start.16
  271.0 1.5 copy-start.3
  271.4 1.3 copy-start.4
  272.7 3.1 copy-start.15
  272.7 3.1 copy-start.17
  275.8 12.3 %copy-start.14 = (s32[128,20]{1,0:T(8,128)}, s32[128,20]{1,0:T(8,128)S(1)}, u32[]{:S(2)}) copy-start(s32[128,20]{1,0:T(8,128)S(1)} %get-tuple-element.541) | copy-start | bytes 30724 | tf_op jit(solution)/shard_map/while
  293.5 2.3 copy-start.16
  299.1 1.5 copy-start.3
  299.5 1.3 copy-start.4
  300.7 3.1 copy-start.15
  300.8 3.1 copy-start.17
  303.8 12.3 %copy-start.14 = (s32[128,20]{1,0:T(8,128)}, s32[128,20]{1,0:T(8,128)S(1)}, u32[]{:S(2)}) copy-start(s32[128,20]{1,0:T(8,128)S(1)} %get-tuple-element.541) | copy-start | bytes 30724 | tf_op jit(solution)/shard_map/while
  321.5 2.3 copy-start.16
  327.1 1.5 copy-start.3
  327.5 1.3 copy-start.4
  328.8 3.1 copy-start.15
  328.8 3.1 copy-start.17
  331.9 12.3 %copy-start.14 = (s32[128,20]{1,0:T(8,128)}, s32[128,20]{1,0:T(8,128)S(1)}, u32[]{:S(2)}) copy-start(s32[128,20]{1,0:T(8,128)S(1)} %get-tuple-element.541) | copy-start | bytes 30724 | tf_op jit(solution)/shard_map/while
  349.6 2.3 copy-start.16
  355.2 1.5 copy-start.3
  355.6 1.3 copy-start.4
  356.9 3.1 copy-start.15
  356.9 3.1 copy-start.17
  362.4 4.3 copy-start.5
  362.4 4.3 copy-start.7
  364.6 159.4 %collective-permute-start.5 = (bf16[2,28,6,640]{3,0,2,1:T(2,128)(2,1)}, bf16[2,28,6,640]{3,0,2,1:T(2,128)(2,1)}, u32[]{:S(2)}, u32[]{:S(2)}) collective-permute-start(bf16[2,28,6,640]{3,0,2,1:T(2,128)(2,1)} %copy.93), channel_id=1, source_target_pairs={{4,0},{8,4},{12,8},{16,12},{20,16},{24,20},{28,24},{0,28},{5,1},{9... | collective-permute-start | bytes 1290248 | tf_op jit(solution)/shard_map/ppermute | solution.py:24
  364.6 160.5 %collective-permute-start.4 = (bf16[2,28,6,640]{3,0,2,1:T(2,128)(2,1)}, bf16[2,28,6,640]{3,0,2,1:T(2,128)(2,1)}, u32[]{:S(2)}, u32[]{:S(2)}) collective-permute-start(bf16[2,28,6,640]{3,0,2,1:T(2,128)(2,1)} %copy.92), channel_id=1, source_target_pairs={{0,4},{4,8},{8,12},{12,16},{16,20},{20,24},{24,28},{28,0},{1,5},{5... | collective-permute-start | bytes 1290248 | tf_op jit(solution)/shard_map/ppermute | solution.py:23
  523.3 2.9 copy-start.6
  523.4 2.9 copy-start.8
  526.3 0.7 copy-start.18
  530.3 254.1 %collective-permute-start.6 = (bf16[2,6,8,640]{3,2,1,0:T(8,128)(2,1)S(1)}, bf16[2,6,8,640]{3,2,1,0:T(8,128)(2,1)S(1)}, u32[]{:S(2)}, u32[]{:S(2)}) collective-permute-start(bf16[2,6,8,640]{3,2,1,0:T(8,128)(2,1)S(1)} %get-tuple-element.364), channel_id=1, source_target_pairs={{0,32},{32,64},{64,96},{96,128},{128,160},{160,192},{192,224},{1,3... | collective-permute-start | bytes 368648 | tf_op jit(solution)/shard_map/ppermute | solution.py:23
  532.2 252.1 %collective-permute-start.7 = (bf16[2,6,8,640]{3,2,1,0:T(8,128)(2,1)S(1)}, bf16[2,6,8,640]{3,2,1,0:T(8,128)(2,1)S(1)}, u32[]{:S(2)}, u32[]{:S(2)}) collective-permute-start(bf16[2,6,8,640]{3,2,1,0:T(8,128)(2,1)S(1)} %get-tuple-element.365), channel_id=1, source_target_pairs={{32,0},{64,32},{96,64},{128,96},{160,128},{192,160},{224,192},{33,... | collective-permute-start | bytes 368648 | tf_op jit(solution)/shard_map/ppermute | solution.py:24
  784.3 1.3 copy-start.10
  784.3 1.3 copy-start.19
  784.3 2.1 copy-start.1
Sparse Core Ops, SparseCore 0:
  9.8 26.8 all-gather.3
  38.5 201.9 all-gather.5
  243.6 492.6 reduce-scatter.1
